TPU v7x, 512 devices: a whole 4x4x16 slice. The times are simulated.
512 devices in a mesh: test: 8 (over z_lo, core), bx: 4 (over y), by: 16 (over z_hi, x).
Axes of the slice: x: 4, y: 4, z: 16 (z_hi: 4, z_lo: 4; z = z_hi * 4 + z_lo), core: 2. Of those that a mesh axis runs over, the one named last changes fastest.
Arguments:
- log_conductivity: float32 [32, 128, 256], P('bx', 'by'), may hold values from -3 to 3
- storage: float32 [32, 128, 256], P('bx', 'by'), may hold values from 0.5 to 2
- recharge: float32 [32, 128, 256], P('bx', 'by'), may hold values from -6 to 6
- pump_rate: float32 [32], P('test'), may hold values from 4 to 16
- pump_well: int32 [32], P('test'), may hold values from 0 to 2047
- observed: float32 [32, 2048], P('test'), may hold values from -9 to 9
- owner: int32 [2048], replicated, may hold values from 0 to 63, as said below
- screen_column: int32 [2048], replicated, may hold values from 0 to 63
- screen_top: int32 [2048], replicated, may hold values from 0 to 248
Outputs:
- gradient: float32 [32, 128, 256], P('bx', 'by', 'test')
Inputs may be any that keep to these rules, and one draw needn't show every extreme that they name: `owner`: each brick owns exactly 32 wells.
All inputs are finite; a program needn't handle non-finite values.
Results may differ from a plain program's by a relative error of at most 0.0001.
Values sent between devices are 32-bit elements; how exact they have to be, the bound alone decides.
A program may use at most 64 MiB of HBM per device.

v0:
```python
import jax
import jax.numpy as jnp
from jax import lax
from jax.sharding import PartitionSpec as P

SWEEPS = 3
SCREEN = 8
epsilon = 1e-06


def with_halo(block, sides, width):
    for axis, dim in sides:
        count = lax.axis_size(axis)
        forward = [(i, i + 1) for i in range(count - 1)]
        backward = [(target, source) for source, target in forward]
        low = lax.ppermute(
            lax.slice_in_dim(block, block.shape[dim] - width, None, axis=dim), axis, forward
        )
        high = lax.ppermute(lax.slice_in_dim(block, 0, width, axis=dim), axis, backward)
        block = jnp.concatenate([low, block, high], axis=dim)
    return block


def pad_depth(values):
    return jnp.pad(values, [(0, 0)] * (values.ndim - 1) + [(1, 1)])


def neighbours(padded, centre):
    z_padded = pad_depth(centre)
    return [
        padded[..., 2:, 1:-1, :],
        padded[..., :-2, 1:-1, :],
        padded[..., 1:-1, 2:, :],
        padded[..., 1:-1, :-2, :],
        z_padded[..., 2:],
        z_padded[..., :-2],
    ]


def weighted(conductance, others):
    accumulated = conductance[0] * others[0]
    for position in range(1, 6):
        accumulated = accumulated + conductance[position] * others[position]
    return accumulated


def sensitivity(conductance, heads_field, heads_padded, adjoint_field, adjoint_padded):
    near_heads = neighbours(heads_padded, heads_field)
    near_adjoint = neighbours(adjoint_padded, adjoint_field)
    accumulated = jnp.zeros_like(heads_field)
    for position in range(6):
        accumulated = accumulated + conductance[position] * (heads_field - near_heads[position]) * (
            adjoint_field - near_adjoint[position]
        )
    return -0.5 * accumulated


def relax_field(source, conductance, diagonal):
    iterate = source / diagonal
    for sweep_index in range(SWEEPS - 1):
        padded = with_halo(iterate, (("bx", 1), ("by", 2)), 1)
        iterate = (source + weighted(conductance, neighbours(padded, iterate))) / diagonal
    return iterate


def per_sweep_terms(
    log_conductivity,
    storage,
    recharge,
    pump_rate,
    pump_well,
    observed,
    owner,
    screen_column,
    screen_top,
):
    size_x, size_y, size_z = log_conductivity.shape
    tests_here = pump_rate.shape[0]
    cell_count = size_x * size_y * size_z
    padded_log = with_halo(log_conductivity, (("bx", 0), ("by", 1)), 1)
    conductance = [
        jnp.exp(0.5 * (log_conductivity + other))
        for other in neighbours(padded_log, log_conductivity)
    ]
    diagonal = storage + weighted(conductance, [1.0] * 6)
    brick_index = lax.axis_index("bx") * lax.axis_size("by") + lax.axis_index("by")
    offsets = jnp.arange(SCREEN, dtype=jnp.int32)
    screen_cells = (screen_column * size_z + screen_top)[:, None] + offsets[None, :]
    owned_here = owner == brick_index
    pump_cells = screen_cells[pump_well]
    pump_value = jnp.where(owner[pump_well] == brick_index, -pump_rate, 0.0)
    test_rows = jnp.arange(tests_here, dtype=jnp.int32)[:, None]
    flat_source = jnp.broadcast_to(recharge.reshape(1, cell_count), (tests_here, cell_count))
    flat_source = flat_source.at[test_rows, pump_cells].add(
        jnp.broadcast_to(pump_value[:, None], pump_cells.shape)
    )
    source = flat_source.reshape(tests_here, size_x, size_y, size_z)
    heads_field = relax_field(source, conductance, diagonal)
    well_heads = jnp.mean(heads_field.reshape(tests_here, cell_count)[:, screen_cells], axis=2)
    residual = jnp.where(owned_here[None, :], well_heads - observed, 0.0)
    well_count = residual.shape[1]
    misfit = lax.psum(jnp.sum(residual * residual, axis=1), ("bx", "by")) / well_count + epsilon
    weights = residual / misfit[:, None]
    values = jnp.broadcast_to(weights[:, :, None], (tests_here, well_count, SCREEN)).reshape(
        tests_here, -1
    )
    adjoint_source = (
        jnp.zeros((tests_here, cell_count), jnp.float32).at[:, screen_cells.reshape(-1)].add(values)
    )
    adjoint_field = relax_field(
        adjoint_source.reshape(tests_here, size_x, size_y, size_z), conductance, diagonal
    )
    stacked = with_halo(
        jnp.concatenate([heads_field, adjoint_field], axis=0), (("bx", 1), ("by", 2)), 1
    )
    test_terms = sensitivity(
        conductance, heads_field, stacked[:tests_here], adjoint_field, stacked[tests_here:]
    )
    return (test_terms, misfit)


def local(
    log_conductivity,
    storage,
    recharge,
    pump_rate,
    pump_well,
    observed,
    owner,
    screen_column,
    screen_top,
):
    size_z = log_conductivity.shape[2]
    tests_here = pump_rate.shape[0]
    test_terms, misfit = per_sweep_terms(
        log_conductivity,
        storage,
        recharge,
        pump_rate,
        pump_well,
        observed,
        owner,
        screen_column,
        screen_top,
    )
    local_sum = jnp.sum(test_terms, axis=0)
    all_tests = tests_here * lax.axis_size("test")
    grand_total = lax.psum(local_sum, "test")
    slab_depth = size_z // lax.axis_size("test")
    gradient = lax.dynamic_slice_in_dim(
        grand_total, lax.axis_index("test") * slab_depth, slab_depth, 2
    )
    return gradient / all_tests


def solution(mesh):
    placed = (
        P("bx", "by", None),
        P("bx", "by", None),
        P("bx", "by", None),
        P("test"),
        P("test"),
        P("test", None),
        P(),
        P(),
        P(),
    )
    return jax.shard_map(
        local, mesh=mesh, in_specs=placed, out_specs=P("bx", "by", "test"), check_vma=False
    )
```

profile of v0, /device:TPU:2, one launch (start us, length us, event | category | flops | bytes accessed | tf_op | source)
XLA Modules:
  0.0 626.8 jit_solution(6473687219000279522)
XLA Ops:
  6.5 0.7 fusion.117
  7.3 3.5 collective-permute-start.1
  10.7 1.3 collective-permute-start
  12.0 0.7 compare_select_fusion.3
  12.7 0.7 multiply_add_fusion
  13.4 0.3 iota_add_fusion
  13.8 0.6 gather_fusion
  14.3 1.3 gather_fusion.1
  15.7 0.8 constant_dynamic-update-slice_fusion.1
  16.6 5.6 collective-permute-start.2
  22.2 1.9 collective-permute-start.3
  24.1 0.7 compare_select_fusion.4
  25.0 0.9 copy.25
  26.0 2.1 scatter_fusion
  28.1 1.2 add_add_fusion
  29.5 1.3 collective-permute-start.4
  30.8 5.2 collective-permute-start.5
  36.0 1.6 collective-permute-done.5
  37.6 3.9 collective-permute-start.6
  41.5 1.9 collective-permute-start.7
  43.4 0.3 compare_select_fusion
  43.8 0.5 reshape.131
  44.3 3.1 collective-permute-done.7
  47.4 0.6 copy-done.12
  48.0 1.1 fusion.9
  49.1 1.3 collective-permute-start.8
  50.4 4.9 collective-permute-start.9
  55.3 1.5 collective-permute-done.9
  56.9 1.9 collective-permute-start.10
  58.8 4.6 collective-permute-start.11
  63.4 0.5 add.270
  64.0 1.1 copy.21
  65.4 4.7 copy.20
  70.1 58.2 %gather_fusion.2 = f32[16384,4]{1,0:T(8,128)} fusion(f32[4,16384]{0,1:T(8,128)} %bitcast.34, s32[16384]{0:T(1024)S(1)} %broadcast_clamp_fusion), kind=kCustom, calls=%fused_computation.2 | custom fusion | bytes 589824 | tf_op jit(solution)/shard_map/gather | solution.py:99
  128.3 13.0 %bitcast_reduce_fusion = f32[2048,4]{1,0:T(8,128)S(1)} fusion(f32[16384,4]{1,0:T(8,128)} %gather_fusion.2), kind=kLoop, calls=%fused_computation.7 | loop fusion | flops 57344 | bytes 294912 | tf_op jit(solution)/shard_map/reduce_sum | solution.py:99
  141.4 0.5 multiply_reduce_fusion
  141.8 0.7 compare_select_fusion.1
  142.5 236.4 %psum.14 = f32[4]{0:T(128)S(1)} all-reduce(f32[4]{0:T(128)S(1)} %multiply_reduce_fusion), channel_id=1, replica_groups=mesh['test'=8,'bx'=4,'by'=16] {'bx','by'}, use_global_device_ids=true, to_apply=%region_3.4 | all-reduce | flops 4 | bytes 32 | tf_op jit(solution)/shard_map/psum | solution.py:102
  378.9 0.4 broadcast_divide_fusion
  379.4 91.6 %scatter_custom_fusion.1 = f32[4,16384]{0,1:T(8,128)} fusion(s32[16384]{0:T(1024)} %bitcast.41, f32[4,2048]{0,1:T(8,128)S(1)} %broadcast_divide_fusion, f32[]{:T(128)} %constant.27.clone.1), kind=kCustom, calls=%fused_computation.5 | custom fusion | flops 65536 | bytes 295424 | tf_op jit(solution)/shard_map/scatter-add | solution.py:108
  471.0 5.2 copy.24
  476.3 1.3 collective-permute-start.12
  477.6 4.5 collective-permute-start.13
  482.1 1.6 collective-permute-done.13
  483.8 4.0 collective-permute-start.14
  487.8 1.9 collective-permute-start.15
  489.7 4.0 collective-permute-done.15
  493.9 1.3 collective-permute-start.16
  495.2 4.9 collective-permute-start.17
  500.1 1.6 collective-permute-done.17
  501.7 1.9 collective-permute-start.18
  503.7 3.9 collective-permute-start.19
  507.6 1.9 collective-permute-done.19
  509.8 1.3 collective-permute-start.20
  511.1 4.9 collective-permute-start.21
  516.0 0.3 collective-permute-done.20
  516.3 1.6 collective-permute-done.21
  518.0 1.9 collective-permute-start.22
  519.9 3.9 collective-permute-start.23
  523.8 0.5 collective-permute-done.22
  524.3 1.9 collective-permute-done.23
  526.2 1.1 fusion.35
  527.4 91.2 %all-reduce.9.cloned.1.call-done = f32[8,8,256]{2,1,0:T(8,128)} async-done(((f32[8,8,256]{2,1,0:T(8,128)}), f32[8,8,256]{2,1,0:T(8,128)}) %all-reduce.9.cloned.1.call-update) | async-done | bytes 65552 | tf_op jit(solution)/shard_map/psum | solution.py:148
  618.5 1.4 dynamic-slice_multiply_fusion
  (67 shorter events, 1.7 us)
Async XLA Ops:
  6.5 56.9 %copy-start = (s32[2048]{0:T(1024)S(1)}, s32[2048]{0:T(1024)}, u32[]{:S(2)}) copy-start(s32[2048]{0:T(1024)} %param.15) | copy-start | bytes 24580
  6.5 612.0 %all-reduce.9.cloned.1.call-start = ((), (), s32[]{:S(2)}) async-start(), calls=%async_computation | async-start | bytes 131072 | tf_op jit(solution)/shard_map/psum | solution.py:148
  7.3 8.4 %collective-permute-start.1 = (f32[1,8,256]{2,1,0:T(8,128)S(1)}, f32[1,8,256]{2,1,0:T(8,128)S(1)}, u32[]{:S(2)}, u32[]{:S(2)}) collective-permute-start(f32[1,8,256]{2,1,0:T(8,128)S(1)} %get-tuple-element.35), channel_id=1, source_target_pairs={{0,16},{16,32},{32,48},{1,17},{17,33},{33,49},{2,18},{18,34},{34,5... | collective-permute-start | bytes 24584 | tf_op jit(solution)/shard_map/ppermute | solution.py:16
  10.7 5.8 collective-permute-start
  16.6 11.5 %collective-permute-start.2 = (f32[10,1,256]{2,1,0:T(1,128)S(1)}, f32[10,1,256]{2,1,0:T(1,128)S(1)}, u32[]{:S(2)}, u32[]{:S(2)}) collective-permute-start(f32[10,1,256]{2,1,0:T(1,128)S(1)} %get-tuple-element.33), channel_id=1, source_target_pairs={{1,0},{2,1},{3,2},{4,3},{5,4},{6,5},{7,6},{8,7},{9,8},{10,9},{11,1... | collective-permute-start | bytes 30728 | tf_op jit(solution)/shard_map/ppermute | solution.py:19
  22.2 5.9 collective-permute-start.3
  29.3 40.8 %copy-start.1 = (f32[8,8,256]{2,1,0:T(8,128)}, f32[8,8,256]{2,1,0:T(8,128)S(1)}, u32[]{:S(2)}) copy-start(f32[8,8,256]{2,1,0:T(8,128)S(1)} %get-tuple-element.7) | copy-start | bytes 196612
  29.3 40.8 %copy-start.3 = (f32[8,8,256]{2,1,0:T(8,128)}, f32[8,8,256]{2,1,0:T(8,128)S(1)}, u32[]{:S(2)}) copy-start(f32[8,8,256]{2,1,0:T(8,128)S(1)} %get-tuple-element.8) | copy-start | bytes 196612
  29.4 40.8 %copy-start.5 = (f32[8,8,256]{2,1,0:T(8,128)}, f32[8,8,256]{2,1,0:T(8,128)S(1)}, u32[]{:S(2)}) copy-start(f32[8,8,256]{2,1,0:T(8,128)S(1)} %get-tuple-element.9) | copy-start | bytes 196612
  29.4 40.8 %copy-start.7 = (f32[8,8,256]{2,1,0:T(8,128)}, f32[8,8,256]{2,1,0:T(8,128)S(1)}, u32[]{:S(2)}) copy-start(f32[8,8,256]{2,1,0:T(8,128)S(1)} %get-tuple-element.10) | copy-start | bytes 196612
  29.4 40.8 %copy-start.9 = (f32[8,8,256]{2,1,0:T(8,128)}, f32[8,8,256]{2,1,0:T(8,128)S(1)}, u32[]{:S(2)}) copy-start(f32[8,8,256]{2,1,0:T(8,128)S(1)} %get-tuple-element.11) | copy-start | bytes 196612
  29.5 6.5 %collective-permute-start.4 = (f32[4,1,8,256]{3,2,1,0:T(8,128)S(1)}, f32[4,1,8,256]{3,2,1,0:T(8,128)S(1)}, u32[]{:S(2)}, u32[]{:S(2)}) collective-permute-start(f32[4,1,8,256]{3,2,1,0:T(8,128)S(1)} %get-tuple-element.31), channel_id=1, source_target_pairs={{16,0},{32,16},{48,32},{17,1},{33,17},{49,33},{18,2},{34,18},{50,3... | collective-permute-start | bytes 98312 | tf_op jit(solution)/shard_map/ppermute | solution.py:19
  30.8 6.8 %collective-permute-start.5 = (f32[4,1,8,256]{3,2,1,0:T(8,128)S(1)}, f32[4,1,8,256]{3,2,1,0:T(8,128)S(1)}, u32[]{:S(2)}, u32[]{:S(2)}) collective-permute-start(f32[4,1,8,256]{3,2,1,0:T(8,128)S(1)} %get-tuple-element.30), channel_id=1, source_target_pairs={{0,16},{16,32},{32,48},{1,17},{17,33},{33,49},{2,18},{18,34},{34,5... | collective-permute-start | bytes 98312 | tf_op jit(solution)/shard_map/ppermute | solution.py:16
  37.6 6.7 %collective-permute-start.6 = (f32[4,10,1,256]{3,2,1,0:T(1,128)S(1)}, f32[4,10,1,256]{3,2,1,0:T(1,128)S(1)}, u32[]{:S(2)}, u32[]{:S(2)}) collective-permute-start(f32[4,10,1,256]{3,2,1,0:T(1,128)S(1)} %get-tuple-element.22), channel_id=1, source_target_pairs={{1,0},{2,1},{3,2},{4,3},{5,4},{6,5},{7,6},{8,7},{9,8},{10,9},{11,1... | collective-permute-start | bytes 122888 | tf_op jit(solution)/shard_map/ppermute | solution.py:19
  41.5 5.9 collective-permute-start.7
  44.3 3.1 copy-start.11
  47.4 0.6 copy-start.12
  49.1 6.2 collective-permute-start.8
  50.4 6.4 %collective-permute-start.9 = (f32[4,1,8,256]{3,2,1,0:T(8,128)S(1)}, f32[4,1,8,256]{3,2,1,0:T(8,128)S(1)}, u32[]{:S(2)}, u32[]{:S(2)}) collective-permute-start(f32[4,1,8,256]{3,2,1,0:T(8,128)S(1)} %get-tuple-element.28), channel_id=1, source_target_pairs={{0,16},{16,32},{32,48},{1,17},{17,33},{33,49},{2,18},{18,34},{34,5... | collective-permute-start | bytes 98312 | tf_op jit(solution)/shard_map/ppermute | solution.py:16
  56.9 8.2 %collective-permute-start.10 = (f32[4,10,1,256]{3,2,1,0:T(1,128)S(1)}, f32[4,10,1,256]{3,2,1,0:T(1,128)S(1)}, u32[]{:S(2)}, u32[]{:S(2)}) collective-permute-start(f32[4,10,1,256]{3,2,1,0:T(1,128)S(1)} %get-tuple-element.20), channel_id=1, source_target_pairs={{1,0},{2,1},{3,2},{4,3},{5,4},{6,5},{7,6},{8,7},{9,8},{10,9},{11,1... | collective-permute-start | bytes 122888 | tf_op jit(solution)/shard_map/ppermute | solution.py:19
  58.8 6.3 %collective-permute-start.11 = (f32[4,10,1,256]{3,2,1,0:T(1,128)S(1)}, f32[4,10,1,256]{3,2,1,0:T(1,128)S(1)}, u32[]{:S(2)}, u32[]{:S(2)}) collective-permute-start(f32[4,10,1,256]{3,2,1,0:T(1,128)S(1)} %get-tuple-element.21), channel_id=1, source_target_pairs={{0,1},{1,2},{2,3},{3,4},{4,5},{5,6},{6,7},{7,8},{8,9},{9,10},{10,1... | collective-permute-start | bytes 122888 | tf_op jit(solution)/shard_map/ppermute | solution.py:16
  379.4 114.3 %copy-start.2 = (f32[8,8,256]{2,1,0:T(8,128)S(1)}, f32[8,8,256]{2,1,0:T(8,128)}, u32[]{:S(2)}) copy-start(f32[8,8,256]{2,1,0:T(8,128)} %copy-done.1) | copy-start | bytes 196612
  379.4 114.3 %copy-start.4 = (f32[8,8,256]{2,1,0:T(8,128)S(1)}, f32[8,8,256]{2,1,0:T(8,128)}, u32[]{:S(2)}) copy-start(f32[8,8,256]{2,1,0:T(8,128)} %copy-done.3) | copy-start | bytes 196612
  379.4 114.3 %copy-start.6 = (f32[8,8,256]{2,1,0:T(8,128)S(1)}, f32[8,8,256]{2,1,0:T(8,128)}, u32[]{:S(2)}) copy-start(f32[8,8,256]{2,1,0:T(8,128)} %copy-done.5) | copy-start | bytes 196612
  379.4 114.3 %copy-start.8 = (f32[8,8,256]{2,1,0:T(8,128)S(1)}, f32[8,8,256]{2,1,0:T(8,128)}, u32[]{:S(2)}) copy-start(f32[8,8,256]{2,1,0:T(8,128)} %copy-done.7) | copy-start | bytes 196612
  379.4 114.3 %copy-start.10 = (f32[8,8,256]{2,1,0:T(8,128)S(1)}, f32[8,8,256]{2,1,0:T(8,128)}, u32[]{:S(2)}) copy-start(f32[8,8,256]{2,1,0:T(8,128)} %copy-done.9) | copy-start | bytes 196612
  476.3 5.9 collective-permute-start.12
  477.6 6.1 collective-permute-start.13
  483.8 5.9 collective-permute-start.14
  487.8 5.9 collective-permute-start.15
  493.9 6.2 collective-permute-start.16
  495.2 6.4 %collective-permute-start.17 = (f32[4,1,8,256]{3,2,1,0:T(8,128)S(1)}, f32[4,1,8,256]{3,2,1,0:T(8,128)S(1)}, u32[]{:S(2)}, u32[]{:S(2)}) collective-permute-start(f32[4,1,8,256]{3,2,1,0:T(8,128)S(1)} %get-tuple-element.24), channel_id=1, source_target_pairs={{0,16},{16,32},{32,48},{1,17},{17,33},{33,49},{2,18},{18,34},{34,5... | collective-permute-start | bytes 98312 | tf_op jit(solution)/shard_map/ppermute | solution.py:16
  501.7 5.9 collective-permute-start.18
  503.7 5.9 collective-permute-start.19
  509.8 6.5 %collective-permute-start.20 = (f32[8,1,8,256]{3,2,1,0:T(8,128)S(1)}, f32[8,1,8,256]{3,2,1,0:T(8,128)S(1)}, u32[]{:S(2)}, u32[]{:S(2)}) collective-permute-start(f32[8,1,8,256]{3,2,1,0:T(8,128)S(1)} %get-tuple-element.15), channel_id=1, source_target_pairs={{16,0},{32,16},{48,32},{17,1},{33,17},{49,33},{18,2},{34,18},{50,3... | collective-permute-start | bytes 196616 | tf_op jit(solution)/shard_map/ppermute | solution.py:19
  511.1 6.7 %collective-permute-start.21 = (f32[8,1,8,256]{3,2,1,0:T(8,128)S(1)}, f32[8,1,8,256]{3,2,1,0:T(8,128)S(1)}, u32[]{:S(2)}, u32[]{:S(2)}) collective-permute-start(f32[8,1,8,256]{3,2,1,0:T(8,128)S(1)} %get-tuple-element.14), channel_id=1, source_target_pairs={{0,16},{16,32},{32,48},{1,17},{17,33},{33,49},{2,18},{18,34},{34,5... | collective-permute-start | bytes 196616 | tf_op jit(solution)/shard_map/ppermute | solution.py:16
  518.0 6.3 %collective-permute-start.22 = (f32[8,10,1,256]{3,2,1,0:T(1,128)S(1)}, f32[8,10,1,256]{3,2,1,0:T(1,128)S(1)}, u32[]{:S(2)}, u32[]{:S(2)}) collective-permute-start(f32[8,10,1,256]{3,2,1,0:T(1,128)S(1)} %get-tuple-element.12), channel_id=1, source_target_pairs={{1,0},{2,1},{3,2},{4,3},{5,4},{6,5},{7,6},{8,7},{9,8},{10,9},{11,1... | collective-permute-start | bytes 245768 | tf_op jit(solution)/shard_map/ppermute | solution.py:19
  519.9 6.3 %collective-permute-start.23 = (f32[8,10,1,256]{3,2,1,0:T(1,128)S(1)}, f32[8,10,1,256]{3,2,1,0:T(1,128)S(1)}, u32[]{:S(2)}, u32[]{:S(2)}) collective-permute-start(f32[8,10,1,256]{3,2,1,0:T(1,128)S(1)} %get-tuple-element.13), channel_id=1, source_target_pairs={{0,1},{1,2},{2,3},{3,4},{4,5},{5,6},{6,7},{7,8},{8,9},{9,10},{10,1... | collective-permute-start | bytes 245768 | tf_op jit(solution)/shard_map/ppermute | solution.py:16
Sparse Core Ops, SparseCore 0:
  527.5 90.9 all-reduce.8
where the time goes:
time: 628 us; the launch traced here: 627 us
  blocking collectives  236 us (38%)
  other arithmetic  117 us (19%)
  waiting for transfers between devices  111 us (18%)
  local copies, waits for them, and re-layouts  75.6 us (12%)
  starting transfers between devices  73 us (12%)
  between operations  14 us (2%)
    psum x1, blocking collectives, per_sweep_terms(): lax.psum(jnp.sum(residual * residual, axis=1), ('bx', 'by')) / well_count  236 us
    scatter-add x1, other arithmetic, per_sweep_terms(): jnp.zeros((tests_here, cell_count), jnp.float32)  91.6 us
    psum x1, waiting for transfers between devices, local(): grand_total = lax.psum(local_sum, 'test')  91.2 us
    gather x1, local copies, waits for them, and re-layouts, per_sweep_terms(): heads_field.reshape(tests_here, cell_count)[:, screen_cells]  58.2 us
    ppermute x12, starting transfers between devices, with_halo(): lax.ppermute(lax.slice_in_dim(block, block.shape[dim] - width, None, axis...  45.9 us
    ppermute x12, starting transfers between devices, with_halo(): lax.ppermute(lax.slice_in_dim(block, 0, width, axis=dim), axis, backward)  27.1 us
    ppermute x12, waiting for transfers between devices, with_halo(): lax.ppermute(lax.slice_in_dim(block, block.shape[dim] - width, None, axis...  18.8 us
    reduce_sum x1, other arithmetic, per_sweep_terms(): jnp.mean(heads_field.reshape(tests_here, cell_count)[:, screen_cells], ax...  13 us
  transfers between devices with their start and end apart: 25, of which 12 were waited for; matrix products, arithmetic and copies ran while one was open for 2% of the time, Pallas kernels for 0%

commit v1 on v0

--- a/solution.py
+++ b/solution.py
@@ -145,7 +145,8 @@
     )
     local_sum = jnp.sum(test_terms, axis=0)
     all_tests = tests_here * lax.axis_size("test")
-    grand_total = lax.psum(local_sum, "test")
+    parts = lax.all_gather(local_sum, "test")
+    grand_total = jnp.sum(parts, axis=0)
     slab_depth = size_z // lax.axis_size("test")
     gradient = lax.dynamic_slice_in_dim(
         grand_total, lax.axis_index("test") * slab_depth, slab_depth, 2

time: 628 us -> 551 us (0.88)
  the two profiles are of different devices: /device:TPU:2 before, /device:TPU:153 now
where the time goes in v1:
time: 551 us; the launch traced here: 549 us
  blocking collectives  216 us (39%)
  other arithmetic  116 us (21%)
  starting transfers between devices  82 us (15%)
  local copies, waits for them, and re-layouts  75.3 us (14%)
  waiting for transfers between devices  60.1 us (11%)
    psum x1, blocking collectives, per_sweep_terms(): lax.psum(jnp.sum(residual * residual, axis=1), ('bx', 'by')) / well_count  157 us
    scatter-add x1, other arithmetic, per_sweep_terms(): jnp.zeros((tests_here, cell_count), jnp.float32)  91.6 us
    ppermute x12, waiting for transfers between devices, with_halo(): lax.ppermute(lax.slice_in_dim(block, block.shape[dim] - width, None, axis...  60.1 us
    ppermute x12, starting transfers between devices, with_halo(): lax.ppermute(lax.slice_in_dim(block, 0, width, axis=dim), axis, backward)  59 us
    all_gather x1, blocking collectives, local(): parts = lax.all_gather(local_sum, 'test')  58.8 us
    gather x1, local copies, waits for them, and re-layouts, per_sweep_terms(): heads_field.reshape(tests_here, cell_count)[:, screen_cells]  57.9 us
    ppermute x12, starting transfers between devices, with_halo(): lax.ppermute(lax.slice_in_dim(block, block.shape[dim] - width, None, axis...  22.9 us
    reduce_sum x1, other arithmetic, per_sweep_terms(): jnp.mean(heads_field.reshape(tests_here, cell_count)[:, screen_cells], ax...  13 us
  transfers between devices with their start and end apart: 24, of which 11 were waited for; matrix products, arithmetic and copies ran while one was open for 2% of the time, Pallas kernels for 0%

profile of v1, /device:TPU:153, one launch (start us, length us, event | category | flops | bytes accessed | tf_op | source)
XLA Modules:
  0.0 549.4 jit_solution(4453964730085220216)
XLA Ops:
  0.0 0.7 fusion.117
  0.7 1.3 collective-permute-start.1
  2.0 4.0 collective-permute-start
  6.0 0.7 compare_select_fusion.3
  6.7 0.7 multiply_add_fusion
  7.4 0.3 iota_add_fusion
  7.7 0.6 gather_fusion
  8.3 1.3 gather_fusion.1
  9.7 0.8 constant_dynamic-update-slice_fusion.1
  10.5 2.6 collective-permute-start.2
  13.1 2.7 collective-permute-start.3
  15.8 0.7 compare_select_fusion.4
  16.7 0.9 copy.25
  17.7 2.1 scatter_fusion
  19.8 3.7 collective-permute-done.3
  23.5 1.2 add_add_fusion
  24.9 2.4 collective-permute-start.4
  27.2 1.3 collective-permute-start.5
  28.6 3.3 collective-permute-done.5
  32.0 4.9 collective-permute-start.6
  36.9 1.9 collective-permute-start.7
  38.8 0.3 compare_select_fusion
  39.1 0.5 reshape.131
  39.6 8.0 %collective-permute-done.7 = f32[4,10,1,256]{3,2,1,0:T(1,128)S(1)} collective-permute-done((f32[4,10,1,256]{3,2,1,0:T(1,128)S(1)}, f32[4,10,1,256]{3,2,1,0:T(1,128)S(1)}, u32[]{:S(2)}, u32[]{:S(2)}) %collective-permute-start.7) | collective-permute-done | bytes 40992 | tf_op jit(solution)/shard_map/ppermute | solution.py:16
  47.6 0.6 copy-done.12
  48.2 1.1 fusion.9
  49.3 2.4 collective-permute-start.8
  51.7 1.3 collective-permute-start.9
  53.0 3.3 collective-permute-done.9
  56.4 1.9 collective-permute-start.10
  58.3 3.4 collective-permute-start.11
  61.7 0.5 add.268
  62.2 1.1 copy.21
  63.4 5.7 %collective-permute-done.11 = f32[4,10,1,256]{3,2,1,0:T(1,128)S(1)} collective-permute-done((f32[4,10,1,256]{3,2,1,0:T(1,128)S(1)}, f32[4,10,1,256]{3,2,1,0:T(1,128)S(1)}, u32[]{:S(2)}, u32[]{:S(2)}) %collective-permute-start.11) | collective-permute-done | bytes 40992 | tf_op jit(solution)/shard_map/ppermute | solution.py:16
  69.4 4.7 copy.20
  74.1 57.9 %gather_fusion.2 = f32[16384,4]{1,0:T(8,128)} fusion(f32[4,16384]{0,1:T(8,128)} %bitcast.35, s32[16384]{0:T(1024)S(1)} %broadcast_clamp_fusion), kind=kCustom, calls=%fused_computation.2 | custom fusion | bytes 589824 | tf_op jit(solution)/shard_map/gather | solution.py:99
  132.0 13.0 %bitcast_reduce_fusion = f32[2048,4]{1,0:T(8,128)S(1)} fusion(f32[16384,4]{1,0:T(8,128)} %gather_fusion.2), kind=kLoop, calls=%fused_computation.7 | loop fusion | flops 57344 | bytes 294912 | tf_op jit(solution)/shard_map/reduce_sum | solution.py:99
  145.0 0.5 multiply_reduce_fusion
  145.4 0.7 compare_select_fusion.1
  146.1 157.0 %psum.7 = f32[4]{0:T(128)S(1)} all-reduce(f32[4]{0:T(128)S(1)} %multiply_reduce_fusion), channel_id=1, replica_groups=mesh['test'=8,'bx'=4,'by'=16] {'bx','by'}, use_global_device_ids=true, to_apply=%region_3.4 | all-reduce | flops 4 | bytes 32 | tf_op jit(solution)/shard_map/psum | solution.py:102
  303.1 0.4 broadcast_divide_fusion
  303.6 91.6 %scatter_custom_fusion.1 = f32[4,16384]{0,1:T(8,128)} fusion(s32[16384]{0:T(1024)} %bitcast.43, f32[4,2048]{0,1:T(8,128)S(1)} %broadcast_divide_fusion, f32[]{:T(128)} %constant.27.clone.1), kind=kCustom, calls=%fused_computation.5 | custom fusion | flops 65536 | bytes 295424 | tf_op jit(solution)/shard_map/scatter-add | solution.py:108
  395.2 5.2 copy.24
  400.5 1.8 collective-permute-start.12
  402.3 1.3 collective-permute-start.13
  403.7 3.3 collective-permute-done.13
  407.1 9.2 %collective-permute-start.14 = (f32[4,10,1,256]{3,2,1,0:T(1,128)S(1)}, f32[4,10,1,256]{3,2,1,0:T(1,128)S(1)}, u32[]{:S(2)}, u32[]{:S(2)}) collective-permute-start(f32[4,10,1,256]{3,2,1,0:T(1,128)S(1)} %get-tuple-element.18), channel_id=1, source_target_pairs={{1,0},{2,1},{3,2},{4,3},{5,4},{6,5},{7,6},{8,7},{9,8},{10,9},{11,1... | collective-permute-start | bytes 122888 | tf_op jit(solution)/shard_map/ppermute | solution.py:19
  416.3 1.9 collective-permute-start.15
  418.3 8.8 %collective-permute-done.15 = f32[4,10,1,256]{3,2,1,0:T(1,128)S(1)} collective-permute-done((f32[4,10,1,256]{3,2,1,0:T(1,128)S(1)}, f32[4,10,1,256]{3,2,1,0:T(1,128)S(1)}, u32[]{:S(2)}, u32[]{:S(2)}) %collective-permute-start.15) | collective-permute-done | bytes 40992 | tf_op jit(solution)/shard_map/ppermute | solution.py:16
  427.4 20.5 %collective-permute-start.16 = (f32[4,1,8,256]{3,2,1,0:T(8,128)S(1)}, f32[4,1,8,256]{3,2,1,0:T(8,128)S(1)}, u32[]{:S(2)}, u32[]{:S(2)}) collective-permute-start(f32[4,1,8,256]{3,2,1,0:T(8,128)S(1)} %get-tuple-element.25), channel_id=1, source_target_pairs={{16,0},{32,16},{48,32},{17,1},{33,17},{49,33},{18,2},{34,18},{50,3... | collective-permute-start | bytes 98312 | tf_op jit(solution)/shard_map/ppermute | solution.py:19
  447.9 1.3 collective-permute-start.17
  449.2 3.4 collective-permute-done.17
  452.6 4.0 collective-permute-start.18
  456.7 1.9 collective-permute-start.19
  458.6 8.8 %collective-permute-done.19 = f32[4,10,1,256]{3,2,1,0:T(1,128)S(1)} collective-permute-done((f32[4,10,1,256]{3,2,1,0:T(1,128)S(1)}, f32[4,10,1,256]{3,2,1,0:T(1,128)S(1)}, u32[]{:S(2)}, u32[]{:S(2)}) %collective-permute-start.19) | collective-permute-done | bytes 40992 | tf_op jit(solution)/shard_map/ppermute | solution.py:16
  467.7 3.4 collective-permute-start.20
  471.1 1.3 collective-permute-start.21
  472.4 3.7 collective-permute-done.21
  476.2 1.9 collective-permute-start.22
  478.1 3.4 collective-permute-start.23
  481.5 7.9 %collective-permute-done.23 = f32[8,10,1,256]{3,2,1,0:T(1,128)S(1)} collective-permute-done((f32[8,10,1,256]{3,2,1,0:T(1,128)S(1)}, f32[8,10,1,256]{3,2,1,0:T(1,128)S(1)}, u32[]{:S(2)}, u32[]{:S(2)}) %collective-permute-start.23) | collective-permute-done | bytes 81952 | tf_op jit(solution)/shard_map/ppermute | solution.py:16
  489.4 0.5 fusion.35
  489.9 58.8 %all-gather = f32[64,8,256]{2,1,0:T(8,128)S(1)} all-gather(f32[8,8,256]{2,1,0:T(8,128)S(1)} %fusion.35), channel_id=2, replica_groups=mesh['test'=8,'bx'=4,'by'=16] {'test'}, dimensions={0}, use_global_device_ids=true | all-gather | bytes 589824 | tf_op jit(solution)/shard_map/all_gather | solution.py:148
  548.7 0.7 dynamic-slice_multiply_fusion
  (66 shorter events, 1.7 us)
Async XLA Ops:
  0.0 61.7 %copy-start = (s32[2048]{0:T(1024)S(1)}, s32[2048]{0:T(1024)}, u32[]{:S(2)}) copy-start(s32[2048]{0:T(1024)} %param.15) | copy-start | bytes 24580
  0.7 8.9 %collective-permute-start.1 = (f32[1,8,256]{2,1,0:T(8,128)S(1)}, f32[1,8,256]{2,1,0:T(8,128)S(1)}, u32[]{:S(2)}, u32[]{:S(2)}) collective-permute-start(f32[1,8,256]{2,1,0:T(8,128)S(1)} %get-tuple-element.35), channel_id=1, source_target_pairs={{0,16},{16,32},{32,48},{1,17},{17,33},{33,49},{2,18},{18,34},{34,5... | collective-permute-start | bytes 24584 | tf_op jit(solution)/shard_map/ppermute | solution.py:16
  2.0 8.5 %collective-permute-start = (f32[1,8,256]{2,1,0:T(8,128)S(1)}, f32[1,8,256]{2,1,0:T(8,128)S(1)}, u32[]{:S(2)}, u32[]{:S(2)}) collective-permute-start(f32[1,8,256]{2,1,0:T(8,128)S(1)} %get-tuple-element.34), channel_id=1, source_target_pairs={{16,0},{32,16},{48,32},{17,1},{33,17},{49,33},{18,2},{34,18},{50,3... | collective-permute-start | bytes 24584 | tf_op jit(solution)/shard_map/ppermute | solution.py:19
  10.5 9.3 %collective-permute-start.2 = (f32[10,1,256]{2,1,0:T(1,128)S(1)}, f32[10,1,256]{2,1,0:T(1,128)S(1)}, u32[]{:S(2)}, u32[]{:S(2)}) collective-permute-start(f32[10,1,256]{2,1,0:T(1,128)S(1)} %get-tuple-element.33), channel_id=1, source_target_pairs={{1,0},{2,1},{3,2},{4,3},{5,4},{6,5},{7,6},{8,7},{9,8},{10,9},{11,1... | collective-permute-start | bytes 30728 | tf_op jit(solution)/shard_map/ppermute | solution.py:19
  13.1 10.4 %collective-permute-start.3 = (f32[10,1,256]{2,1,0:T(1,128)S(1)}, f32[10,1,256]{2,1,0:T(1,128)S(1)}, u32[]{:S(2)}, u32[]{:S(2)}) collective-permute-start(f32[10,1,256]{2,1,0:T(1,128)S(1)} %get-tuple-element.32), channel_id=1, source_target_pairs={{0,1},{1,2},{2,3},{3,4},{4,5},{5,6},{6,7},{7,8},{8,9},{9,10},{10,1... | collective-permute-start | bytes 30728 | tf_op jit(solution)/shard_map/ppermute | solution.py:16
  24.7 49.3 %copy-start.1 = (f32[8,8,256]{2,1,0:T(8,128)}, f32[8,8,256]{2,1,0:T(8,128)S(1)}, u32[]{:S(2)}) copy-start(f32[8,8,256]{2,1,0:T(8,128)S(1)} %get-tuple-element.7) | copy-start | bytes 196612
  24.8 49.3 %copy-start.3 = (f32[8,8,256]{2,1,0:T(8,128)}, f32[8,8,256]{2,1,0:T(8,128)S(1)}, u32[]{:S(2)}) copy-start(f32[8,8,256]{2,1,0:T(8,128)S(1)} %get-tuple-element.8) | copy-start | bytes 196612
  24.8 49.3 %copy-start.5 = (f32[8,8,256]{2,1,0:T(8,128)}, f32[8,8,256]{2,1,0:T(8,128)S(1)}, u32[]{:S(2)}) copy-start(f32[8,8,256]{2,1,0:T(8,128)S(1)} %get-tuple-element.9) | copy-start | bytes 196612
  24.8 49.3 %copy-start.7 = (f32[8,8,256]{2,1,0:T(8,128)}, f32[8,8,256]{2,1,0:T(8,128)S(1)}, u32[]{:S(2)}) copy-start(f32[8,8,256]{2,1,0:T(8,128)S(1)} %get-tuple-element.10) | copy-start | bytes 196612
  24.8 49.3 %copy-start.9 = (f32[8,8,256]{2,1,0:T(8,128)}, f32[8,8,256]{2,1,0:T(8,128)S(1)}, u32[]{:S(2)}) copy-start(f32[8,8,256]{2,1,0:T(8,128)S(1)} %get-tuple-element.11) | copy-start | bytes 196612
  24.9 3.7 collective-permute-start.4
  27.2 4.7 collective-permute-start.5
  32.0 7.7 %collective-permute-start.6 = (f32[4,10,1,256]{3,2,1,0:T(1,128)S(1)}, f32[4,10,1,256]{3,2,1,0:T(1,128)S(1)}, u32[]{:S(2)}, u32[]{:S(2)}) collective-permute-start(f32[4,10,1,256]{3,2,1,0:T(1,128)S(1)} %get-tuple-element.22), channel_id=1, source_target_pairs={{1,0},{2,1},{3,2},{4,3},{5,4},{6,5},{7,6},{8,7},{9,8},{10,9},{11,1... | collective-permute-start | bytes 122888 | tf_op jit(solution)/shard_map/ppermute | solution.py:19
  36.9 10.8 %collective-permute-start.7 = (f32[4,10,1,256]{3,2,1,0:T(1,128)S(1)}, f32[4,10,1,256]{3,2,1,0:T(1,128)S(1)}, u32[]{:S(2)}, u32[]{:S(2)}) collective-permute-start(f32[4,10,1,256]{3,2,1,0:T(1,128)S(1)} %get-tuple-element.23), channel_id=1, source_target_pairs={{0,1},{1,2},{2,3},{3,4},{4,5},{5,6},{6,7},{7,8},{8,9},{9,10},{10,1... | collective-permute-start | bytes 122888 | tf_op jit(solution)/shard_map/ppermute | solution.py:16
  39.6 8.0 %copy-start.11 = (f32[4,10,1,256]{3,2,1,0:T(1,128)}, f32[4,10,1,256]{3,2,1,0:T(1,128)S(1)}, u32[]{:S(2)}) copy-start(f32[4,10,1,256]{3,2,1,0:T(1,128)S(1)} %collective-permute-done.6) | copy-start | bytes 122884
  47.6 0.6 copy-start.12
  49.3 3.7 collective-permute-start.8
  51.7 4.7 collective-permute-start.9
  56.4 7.0 %collective-permute-start.10 = (f32[4,10,1,256]{3,2,1,0:T(1,128)S(1)}, f32[4,10,1,256]{3,2,1,0:T(1,128)S(1)}, u32[]{:S(2)}, u32[]{:S(2)}) collective-permute-start(f32[4,10,1,256]{3,2,1,0:T(1,128)S(1)} %get-tuple-element.20), channel_id=1, source_target_pairs={{1,0},{2,1},{3,2},{4,3},{5,4},{6,5},{7,6},{8,7},{9,8},{10,9},{11,1... | collective-permute-start | bytes 122888 | tf_op jit(solution)/shard_map/ppermute | solution.py:19
  58.3 10.8 %collective-permute-start.11 = (f32[4,10,1,256]{3,2,1,0:T(1,128)S(1)}, f32[4,10,1,256]{3,2,1,0:T(1,128)S(1)}, u32[]{:S(2)}, u32[]{:S(2)}) collective-permute-start(f32[4,10,1,256]{3,2,1,0:T(1,128)S(1)} %get-tuple-element.21), channel_id=1, source_target_pairs={{0,1},{1,2},{2,3},{3,4},{4,5},{5,6},{6,7},{7,8},{8,9},{9,10},{10,1... | collective-permute-start | bytes 122888 | tf_op jit(solution)/shard_map/ppermute | solution.py:16
  303.6 123.5 %copy-start.2 = (f32[8,8,256]{2,1,0:T(8,128)S(1)}, f32[8,8,256]{2,1,0:T(8,128)}, u32[]{:S(2)}) copy-start(f32[8,8,256]{2,1,0:T(8,128)} %copy-done.1) | copy-start | bytes 196612
  303.6 123.5 %copy-start.4 = (f32[8,8,256]{2,1,0:T(8,128)S(1)}, f32[8,8,256]{2,1,0:T(8,128)}, u32[]{:S(2)}) copy-start(f32[8,8,256]{2,1,0:T(8,128)} %copy-done.3) | copy-start | bytes 196612
  303.6 123.5 %copy-start.6 = (f32[8,8,256]{2,1,0:T(8,128)S(1)}, f32[8,8,256]{2,1,0:T(8,128)}, u32[]{:S(2)}) copy-start(f32[8,8,256]{2,1,0:T(8,128)} %copy-done.5) | copy-start | bytes 196612
  303.6 123.5 %copy-start.8 = (f32[8,8,256]{2,1,0:T(8,128)S(1)}, f32[8,8,256]{2,1,0:T(8,128)}, u32[]{:S(2)}) copy-start(f32[8,8,256]{2,1,0:T(8,128)} %copy-done.7) | copy-start | bytes 196612
  303.6 123.5 %copy-start.10 = (f32[8,8,256]{2,1,0:T(8,128)S(1)}, f32[8,8,256]{2,1,0:T(8,128)}, u32[]{:S(2)}) copy-start(f32[8,8,256]{2,1,0:T(8,128)} %copy-done.9) | copy-start | bytes 196612
  400.5 3.2 collective-permute-start.12
  402.3 4.7 collective-permute-start.13
  407.1 11.2 %collective-permute-start.14 = (f32[4,10,1,256]{3,2,1,0:T(1,128)S(1)}, f32[4,10,1,256]{3,2,1,0:T(1,128)S(1)}, u32[]{:S(2)}, u32[]{:S(2)}) collective-permute-start(f32[4,10,1,256]{3,2,1,0:T(1,128)S(1)} %get-tuple-element.18), channel_id=1, source_target_pairs={{1,0},{2,1},{3,2},{4,3},{5,4},{6,5},{7,6},{8,7},{9,8},{10,9},{11,1... | collective-permute-start | bytes 122888 | tf_op jit(solution)/shard_map/ppermute | solution.py:19
  416.3 10.8 %collective-permute-start.15 = (f32[4,10,1,256]{3,2,1,0:T(1,128)S(1)}, f32[4,10,1,256]{3,2,1,0:T(1,128)S(1)}, u32[]{:S(2)}, u32[]{:S(2)}) collective-permute-start(f32[4,10,1,256]{3,2,1,0:T(1,128)S(1)} %get-tuple-element.19), channel_id=1, source_target_pairs={{0,1},{1,2},{2,3},{3,4},{4,5},{5,6},{6,7},{7,8},{8,9},{9,10},{10,1... | collective-permute-start | bytes 122888 | tf_op jit(solution)/shard_map/ppermute | solution.py:16
  427.4 21.9 %collective-permute-start.16 = (f32[4,1,8,256]{3,2,1,0:T(8,128)S(1)}, f32[4,1,8,256]{3,2,1,0:T(8,128)S(1)}, u32[]{:S(2)}, u32[]{:S(2)}) collective-permute-start(f32[4,1,8,256]{3,2,1,0:T(8,128)S(1)} %get-tuple-element.25), channel_id=1, source_target_pairs={{16,0},{32,16},{48,32},{17,1},{33,17},{49,33},{18,2},{34,18},{50,3... | collective-permute-start | bytes 98312 | tf_op jit(solution)/shard_map/ppermute | solution.py:19
  447.9 4.7 collective-permute-start.17
  452.6 6.0 %collective-permute-start.18 = (f32[4,10,1,256]{3,2,1,0:T(1,128)S(1)}, f32[4,10,1,256]{3,2,1,0:T(1,128)S(1)}, u32[]{:S(2)}, u32[]{:S(2)}) collective-permute-start(f32[4,10,1,256]{3,2,1,0:T(1,128)S(1)} %get-tuple-element.16), channel_id=1, source_target_pairs={{1,0},{2,1},{3,2},{4,3},{5,4},{6,5},{7,6},{8,7},{9,8},{10,9},{11,1... | collective-permute-start | bytes 122888 | tf_op jit(solution)/shard_map/ppermute | solution.py:19
  456.7 10.8 %collective-permute-start.19 = (f32[4,10,1,256]{3,2,1,0:T(1,128)S(1)}, f32[4,10,1,256]{3,2,1,0:T(1,128)S(1)}, u32[]{:S(2)}, u32[]{:S(2)}) collective-permute-start(f32[4,10,1,256]{3,2,1,0:T(1,128)S(1)} %get-tuple-element.17), channel_id=1, source_target_pairs={{0,1},{1,2},{2,3},{3,4},{4,5},{5,6},{6,7},{7,8},{8,9},{9,10},{10,1... | collective-permute-start | bytes 122888 | tf_op jit(solution)/shard_map/ppermute | solution.py:16
  467.7 4.7 collective-permute-start.20
  471.1 5.0 collective-permute-start.21
  476.2 5.3 collective-permute-start.22
  478.1 11.3 %collective-permute-start.23 = (f32[8,10,1,256]{3,2,1,0:T(1,128)S(1)}, f32[8,10,1,256]{3,2,1,0:T(1,128)S(1)}, u32[]{:S(2)}, u32[]{:S(2)}) collective-permute-start(f32[8,10,1,256]{3,2,1,0:T(1,128)S(1)} %get-tuple-element.13), channel_id=1, source_target_pairs={{0,1},{1,2},{2,3},{3,4},{4,5},{5,6},{6,7},{7,8},{8,9},{9,10},{10,1... | collective-permute-start | bytes 245768 | tf_op jit(solution)/shard_map/ppermute | solution.py:16
